TPU v7x, 128 devices: a whole 4x4x4 slice. The times are simulated.
128 devices in a mesh: grp: 2 (over x_hi), layer: 4 (over z), feat: 16 (over x_lo, y, core).
Axes of the slice: x: 4 (x_hi: 2, x_lo: 2; x = x_hi * 2 + x_lo), y: 4, z: 4, core: 2. Of those that a mesh axis runs over, the one named last changes fastest.
Arguments:
- inputs: bfloat16 [4, 2048, 2304], P('layer', ('grp', 'feat')), may hold values from -6 to 6
- targets: bfloat16 [2048, 4, 2304], P(('grp', 'feat'), None, 'layer'), may hold values from -6 to 6
- enc_weight: bfloat16 [4, 2304, 8192], P('layer', None, 'feat'), may hold values from -0.125 to 0.125
- enc_bias: float32 [4, 8192], P('layer', 'feat'), may hold values from -3 to 3
- dec_weight: bfloat16 [10, 8192, 2304], P(None, 'feat', 'layer'), may hold values from -0.0625 to 0.0625
- dec_bias: float32 [4, 2304], P(None, 'layer'), may hold values from -3 to 3
Outputs:
- enc_grad: bfloat16 [4, 2304, 8192], P('layer', 'grp', 'feat')
- enc_bias_grad: float32 [4, 8192], P('layer', 'feat')
- dec_grad: bfloat16 [10, 8192, 2304], P('grp', 'feat', 'layer')
- dec_bias_grad: float32 [4, 2304], P(None, 'layer')
All inputs are finite; a program needn't handle non-finite values.
Results may differ from a plain program's by a relative error of at most 0.019.
Values may be sent and summed in bfloat16 or wider, within the bound.
No kernel may reach another device: no remote copies, remote signals or barrier semaphores. Data moves between devices by JAX's collectives and lax.ppermute only.
A program may use at most 128 MiB of HBM per device.

v0:
```python
import jax
import jax.numpy as jnp
from jax import lax
from jax.sharding import Mesh
from jax.sharding import PartitionSpec as P

FEAT = ("feat_0", "feat_1", "feat_2")
GRP_FEAT = ("grp", "feat_0", "feat_1", "feat_2")


def cut_along(x, dim, size):
    before, after = (x.shape[:dim], x.shape[dim + 1 :])
    return jnp.moveaxis(x.reshape(*before, size, -1, *after), dim, 0)


def summed_rows_2(x, chips, core, dim):
    sizes = (lax.axis_size(chips), lax.axis_size(core))
    blocks = cut_along(x, dim, sizes[0] * sizes[1])
    inside = blocks.shape[1:]
    blocks = blocks.reshape(*sizes, *inside).swapaxes(0, 1).reshape(-1, *inside)
    blocks = lax.psum_scatter(blocks, core, scatter_dimension=0, tiled=True)
    return lax.psum_scatter(blocks, chips, scatter_dimension=0, tiled=True)[0]


def sent_to_all(x, axis):
    copies = jnp.broadcast_to(x, (lax.axis_size(axis), *x.shape))
    return lax.all_to_all(copies, axis, split_axis=0, concat_axis=0, tiled=True)


def taken_together(x, axis):
    everything = sent_to_all(x, axis)
    return jnp.sum(everything, axis=0)


def sent_and_summed(x, axis, dim):
    blocks = cut_along(x, dim, lax.axis_size(axis))
    arrived = lax.all_to_all(blocks, axis, split_axis=0, concat_axis=0, tiled=True)
    return arrived.astype(jnp.float32).sum(axis=0)


def pair_list(count):
    return [(source, target) for source in range(count) for target in range(source, count)]


def per_device(inputs, targets, enc_weight, enc_bias, dec_weight, dec_bias):
    layers = lax.axis_size("layer")
    feat_count = lax.axis_size(FEAT)
    group_count = lax.axis_size("grp")
    pairs = pair_list(layers)
    tok_dev = inputs.shape[1]
    total_tokens = tok_dev * feat_count * group_count
    rows = lax.all_gather(inputs[0], FEAT, axis=0, tiled=True)
    pre = jnp.dot(rows, enc_weight[0], preferred_element_type=jnp.float32) + enc_bias[0]
    acts = jnp.maximum(pre, 0.0).astype(jnp.bfloat16)
    sources = lax.all_gather(acts[None], "layer", axis=0, tiled=True)

    def decode_target(block, target):
        total = jnp.zeros((block.shape[1], dec_weight.shape[2]), jnp.float32)
        for index, (source, later) in enumerate(pairs):
            if later == target:
                total = total + jnp.dot(
                    block[source], dec_weight[index], preferred_element_type=jnp.float32
                )
        return total

    def partial_rows():
        return jnp.stack([decode_target(sources, target) for target in range(layers)], axis=1)

    recon = summed_rows_2(
        partial_rows().astype(jnp.bfloat16), ("feat_0", "feat_1"), "feat_2", 0
    ).astype(jnp.float32)
    errors = recon + dec_bias - targets.astype(jnp.float32)
    dec_bias_grad = taken_together(jnp.sum(errors, axis=0), GRP_FEAT) / total_tokens
    derr = lax.all_gather((errors / total_tokens).astype(jnp.bfloat16), FEAT, axis=0, tiled=True)
    terms = jnp.stack(
        [
            jnp.einsum("rf,rd->fd", sources[s], derr[:, t, :], preferred_element_type=jnp.float32)
            for s, t in pairs
        ]
    )
    dec_grad = lax.psum_scatter(terms.astype(jnp.bfloat16), "grp", scatter_dimension=0, tiled=True)
    partials = []
    for source in range(layers):
        total = jnp.zeros((derr.shape[0], dec_weight.shape[1]), jnp.float32)
        for index, (first, target) in enumerate(pairs):
            if first == source:
                total = total + jnp.einsum(
                    "rd,fd->rf",
                    derr[:, target, :],
                    dec_weight[index],
                    preferred_element_type=jnp.float32,
                )
        partials.append(total)
    dacts = lax.psum_scatter(
        jnp.stack(partials).astype(jnp.bfloat16), "layer", scatter_dimension=0, tiled=True
    ).astype(jnp.float32)[0]
    dpre = jnp.where(pre > 0, dacts, jnp.zeros_like(dacts))
    enc_bias_grad = taken_together(jnp.sum(dpre, axis=0), "grp")[None]
    dpre_half = dpre.astype(jnp.bfloat16)
    block = rows
    enc_grad = sent_and_summed(
        jnp.einsum("rd,rf->df", block, dpre_half, preferred_element_type=jnp.float32).astype(
            jnp.bfloat16
        ),
        "grp",
        0,
    ).astype(jnp.bfloat16)[None]
    return (enc_grad, enc_bias_grad, dec_grad, dec_bias_grad)


def solution(mesh):
    finer = Mesh(
        mesh.devices.reshape(mesh.shape["grp"], mesh.shape["layer"], 2, 4, 2),
        ("grp", "layer", "feat_0", "feat_1", "feat_2"),
    )
    placed = (
        P("layer", GRP_FEAT, None),
        P(GRP_FEAT, None, "layer"),
        P("layer", None, FEAT),
        P("layer", FEAT),
        P(None, FEAT, "layer"),
        P(None, "layer"),
    )
    return jax.shard_map(
        per_device,
        mesh=finer,
        in_specs=placed,
        out_specs=(
            P("layer", "grp", FEAT),
            P("layer", FEAT),
            P("grp", FEAT, "layer"),
            P(None, "layer"),
        ),
        check_vma=False,
    )
```

profile of v0, /device:TPU:0, one launch (start us, length us, event | category | flops | bytes accessed | tf_op | source)
XLA Modules:
  0.0 419.8 jit_solution(11009269776554832123)
XLA Ops:
  7.2 0.7 all-gather.8.cloned.1.call-update
  8.0 42.8 %all-gather.8.cloned.1.call-done = bf16[1,1024,2304]{2,1,0:T(8,128)(2,1)} async-done(((bf16[1,64,2304]{2,1,0:T(8,128)(2,1)}), bf16[1,1024,2304]{2,1,0:T(8,128)(2,1)}) %all-gather.8.cloned.1.call-update) | async-done | bytes 4718608 | tf_op jit(solution)/shard_map/all_gather | solution.py:52
  50.8 6.6 %maximum_convert_fusion = (bf16[1024,512]{1,0:T(8,128)(2,1)}, f32[1024,512]{1,0:T(8,128)}) fusion(f32[512]{0:T(512)} %bitcast.205, bf16[1,2304,512]{2,1,0:T(8,128)(2,1)S(1)} %copy-done, bf16[1,1024,2304]{2,1,0:T(8,128)(2,1)} %all-gather.8.cloned.1.call-done), kind=kOutput, calls=%fused_computation.18 | convolution fusion | flops 2417491968 | bytes 10225664 | tf_op jit(solution)/shard_map/dot_general | solution.py:53
  57.4 0.0 reduce-scatter.5.cloned.1.call-start
  57.4 48.6 %all-gather.10.cloned.1.call-done = bf16[4096,512]{1,0:T(8,128)(2,1)} async-done(((bf16[1024,512]{1,0:T(8,128)(2,1)}), bf16[4096,512]{1,0:T(8,128)(2,1)}) %all-gather.10.cloned.1.call-update) | async-done | bytes 4194320 | tf_op jit(solution)/shard_map/all_gather | solution.py:55
  106.1 1.4 slice.58
  107.5 3.3 fusion.10
  110.8 1.9 fusion.74
  112.7 1.9 add_convert_fusion.2
  114.6 1.5 copy.46
  116.1 2.2 fusion.69
  118.3 2.2 fusion.65
  120.4 2.3 add_convert_fusion.1
  122.7 1.4 copy.47
  124.2 2.3 fusion.58
  126.5 2.2 fusion.55
  128.7 1.9 fusion.44
  130.6 2.1 add_convert_fusion
  132.7 0.7 copy.48
  133.4 2.6 maximum_bitcast_fusion
  136.0 2.9 copy.49
  139.0 0.0 reduce-scatter.7.cloned.1.call-start
  139.1 16.0 %reduce-scatter.5.cloned.1.call-done = bf16[8,64,4,576]{3,1,2,0:T(8,128)(2,1)} async-done(((bf16[16,64,4,576]{3,1,2,0:T(8,128)(2,1)}), bf16[8,64,4,576]{3,1,2,0:T(8,128)(2,1)}) %reduce-scatter.5.cloned.1.call-update) | async-done | bytes 2359312 | tf_op jit(solution)/shard_map/reduce_scatter | solution.py:21
  155.1 48.1 %reduce-scatter.7.cloned.1.call-done = bf16[1,64,4,576]{3,1,2,0:T(8,128)(2,1)} async-done(((bf16[8,64,4,576]{3,1,2,0:T(8,128)(2,1)}), bf16[1,64,4,576]{3,1,2,0:T(8,128)(2,1)}) %reduce-scatter.7.cloned.1.call-update) | async-done | bytes 294928 | tf_op jit(solution)/shard_map/reduce_scatter | solution.py:22
  203.2 1.8 fusion.77
  205.1 0.2 reduce-scatter.9.cloned.1.call-start
  205.3 38.8 %all-gather.6.cloned.1.call-done = bf16[1024,4,576]{2,0,1:T(8,128)(2,1)} async-done(((bf16[64,4,576]{2,0,1:T(8,128)(2,1)}), bf16[1024,4,576]{2,0,1:T(8,128)(2,1)}) %all-gather.6.cloned.1.call-update) | async-done | bytes 4718608 | tf_op jit(solution)/shard_map/all_gather | solution.py:74
  244.1 2.6 fusion.11
  246.7 2.6 fusion.63
  249.3 2.4 fusion.60
  251.8 1.0 fusion.41
  252.7 1.0 fusion.67
  253.7 1.0 fusion.42
  254.7 1.0 fusion.35
  255.7 1.0 fusion.14
  256.7 1.0 fusion.13
  257.6 1.0 fusion.12
  258.6 2.2 pad_maximum_fusion
  260.9 3.4 fusion.16
  264.3 3.1 fusion.18
  267.4 3.0 fusion.20
  270.4 1.6 fusion.22
  272.0 1.6 fusion.24
  273.6 1.6 fusion.26
  275.2 1.6 fusion.28
  276.9 1.6 fusion.30
  278.5 1.6 fusion.32
  280.1 1.6 fusion.34
  281.8 0.8 broadcast_in_dim.20
  282.5 6.0 %all-to-all-start.2 = ((f32[32,4,576]{2,1,0:T(4,128)}), f32[32,4,576]{2,1,0:T(4,128)S(1)}, u32[]{:S(2)}, u32[]{:S(2)}) async-start(f32[32,4,576]{2,1,0:T(4,128)} %broadcast_in_dim.20), calls=%async_computation.6 | async-start | bytes 655360 | tf_op jit(solution)/shard_map/all_to_all | solution.py:27
  288.5 19.7 %reduce-scatter.9.cloned.1.call-done = bf16[1,1024,512]{2,1,0:T(8,128)(2,1)} async-done(((bf16[4,1024,512]{2,1,0:T(8,128)(2,1)}), bf16[1,1024,512]{2,1,0:T(8,128)(2,1)}) %reduce-scatter.9.cloned.1.call-update) | async-done | bytes 1048592 | tf_op jit(solution)/shard_map/reduce_scatter | solution.py:94
  308.2 1.8 fusion.8
  310.0 0.6 broadcast_in_dim.18
  310.6 4.3 %all-to-all-start.1 = ((f32[2,1,512]{2,1,0:T(1,128)}), f32[2,1,512]{2,1,0:T(1,128)S(1)}, u32[]{:S(2)}, u32[]{:S(2)}) async-start(f32[2,1,512]{2,1,0:T(1,128)} %broadcast_in_dim.18), calls=%async_computation.4 | async-start | bytes 8192 | tf_op jit(solution)/shard_map/all_to_all | solution.py:27
  314.9 5.3 %fusion.4 = bf16[512,2304]{1,0:T(8,128)(2,1)S(1)} fusion(bf16[1,1024,2304]{2,1,0:T(8,128)(2,1)} %all-gather.8.cloned.1.call-done, pred[1024,512]{1,0:T(32,128)(4,1)S(1)} %get-tuple-element.17, bf16[1,1024,512]{2,1,0:T(8,128)(2,1)} %reduce-scatter.9.cloned.1.call-done), kind=kOutput, calls=%fused_computation.5 | convolution fusion | flops 2418671616 | bytes 8650752 | tf_op jit(solution)/shard_map/rd,rf->df/dot_general | solution.py:102
  320.2 1.7 copy.68
  321.8 4.9 %all-to-all-start = ((bf16[2,1152,512]{1,2,0:T(8,128)(2,1)}), bf16[2,1152,512]{1,2,0:T(8,128)(2,1)}, u32[]{:S(2)}, u32[]{:S(2)}) async-start(bf16[2,1152,512]{1,2,0:T(8,128)(2,1)} %bitcast.194), calls=%async_computation.3 | async-start | bytes 4718592 | tf_op jit(solution)/shard_map/all_to_all | solution.py:37
  326.8 0.1 reduce_sum.52
  326.9 0.6 broadcast_multiply_fusion
  327.5 0.6 reduce_sum.50
  328.1 54.2 %all-to-all-done = bf16[2,1152,512]{1,2,0:T(8,128)(2,1)} async-done(((bf16[2,1152,512]{1,2,0:T(8,128)(2,1)}), bf16[2,1152,512]{1,2,0:T(8,128)(2,1)}, u32[]{:S(2)}, u32[]{:S(2)}) %all-to-all-start) | async-done | bytes 2359328 | tf_op jit(solution)/shard_map/all_to_all | solution.py:37
  382.2 2.8 reduce_sum.48
  385.0 1.4 copy.59
  386.4 26.5 %reduce-scatter.11.cloned.1.call-done = bf16[5,512,576]{1,2,0:T(8,128)(2,1)} async-done(((bf16[10,512,576]{1,2,0:T(8,128)(2,1)}), bf16[5,512,576]{1,2,0:T(8,128)(2,1)}) %reduce-scatter.11.cloned.1.call-update) | async-done | bytes 2949136 | tf_op jit(solution)/shard_map/reduce_scatter | solution.py:81
  (42 shorter events, 0.3 us)
Async XLA Ops:
  7.2 43.6 %copy-start = (bf16[1,2304,512]{2,1,0:T(8,128)(2,1)S(1)}, bf16[1,2304,512]{2,1,0:T(8,128)(2,1)}, u32[]{:S(2)}) copy-start(bf16[1,2304,512]{2,1,0:T(8,128)(2,1)} %param.8) | copy-start | bytes 7077892
  7.2 43.6 %all-gather.8.cloned.1.call-start = ((), (), s32[]{:S(2)}) async-start(), calls=%async_computation.12 | async-start | bytes 5013504 | tf_op jit(solution)/shard_map/all_gather | solution.py:52
  7.9 98.2 %all-gather.10.cloned.1.call-start = ((), (), s32[]{:S(2)}) async-start(), calls=%async_computation.13 | async-start | bytes 5242880 | tf_op jit(solution)/shard_map/all_gather | solution.py:55
  57.4 97.7 %reduce-scatter.5.cloned.1.call-start = ((), (), s32[]{:S(2)}) async-start(), calls=%async_computation.7 | async-start | bytes 7864320 | tf_op jit(solution)/shard_map/reduce_scatter | solution.py:21
  106.1 4.8 %copy-start.2 = (bf16[4096,512]{1,0:T(8,128)(2,1)S(1)}, bf16[4096,512]{1,0:T(8,128)(2,1)}, u32[]{:S(2)}) copy-start(bf16[4096,512]{1,0:T(8,128)(2,1)} %all-gather.10.cloned.1.call-done) | copy-start | bytes 12582916
  124.2 4.5 %copy-start.3 = (bf16[4096,512]{1,0:T(8,128)(2,1)S(1)}, bf16[4096,512]{1,0:T(8,128)(2,1)}, u32[]{:S(2)}) copy-start(bf16[4096,512]{1,0:T(8,128)(2,1)} %all-gather.10.cloned.1.call-done) | copy-start | bytes 12582916
  139.0 64.2 %copy-start.7 = (bf16[64,4,576]{2,1,0:T(4,128)(2,1)S(1)}, bf16[64,4,576]{2,1,0:T(4,128)(2,1)}, u32[]{:S(2)}) copy-start(bf16[64,4,576]{2,1,0:T(4,128)(2,1)} %param.7) | copy-start | bytes 884740
  139.0 64.2 %copy-start.8 = (f32[4,576]{1,0:T(4,128)S(1)}, f32[4,576]{1,0:T(4,128)}, u32[]{:S(2)}) copy-start(f32[4,576]{1,0:T(4,128)} %param.11) | copy-start | bytes 27652
  139.0 64.2 %reduce-scatter.7.cloned.1.call-start = ((), (), s32[]{:S(2)}) async-start(), calls=%async_computation.8 | async-start | bytes 2949120 | tf_op jit(solution)/shard_map/reduce_scatter | solution.py:22
  155.1 89.0 %all-gather.6.cloned.1.call-start = ((), (), s32[]{:S(2)}) async-start(), calls=%async_computation.9 | async-start | bytes 5570560 | tf_op jit(solution)/shard_map/all_gather | solution.py:74
  205.1 103.1 %reduce-scatter.9.cloned.1.call-start = ((), (), s32[]{:S(2)}) async-start(), calls=%async_computation.10 | async-start | bytes 5242880 | tf_op jit(solution)/shard_map/reduce_scatter | solution.py:94
  244.1 7.6 %slice-start = ((s8[5898240]{0:T(1024)(128)(4,1)}), s8[4194304]{0:T(1024)(128)(4,1)S(1)}, s32[]{:S(2)}) async-start(s8[5898240]{0:T(1024)(128)(4,1)} %bitcast.195), calls=%async_computation.14 | async-start | bytes 8388608
  246.7 5.1 %slice-start.1 = ((s8[5898240]{0:T(1024)(128)(4,1)}), s8[1703936]{0:T(1024)(128)(4,1)S(1)}, s32[]{:S(2)}) async-start(s8[5898240]{0:T(1024)(128)(4,1)} %bitcast.195), calls=%async_computation.15 | async-start | bytes 3407872
  246.7 5.0 %copy-start.5 = (bf16[1024,4,576]{2,0,1:T(8,128)(2,1)S(1)}, bf16[1024,4,576]{2,0,1:T(8,128)(2,1)}, u32[]{:S(2)}) copy-start(bf16[1024,4,576]{2,0,1:T(8,128)(2,1)} %all-gather.6.cloned.1.call-done) | copy-start | bytes 14155780
  260.9 152.0 %reduce-scatter.11.cloned.1.call-start = ((), (), s32[]{:S(2)}) async-start(), calls=%async_computation.11 | async-start | bytes 8847360 | tf_op jit(solution)/shard_map/reduce_scatter | solution.py:81
  260.9 3.4 copy-start.4
  260.9 9.4 %slice-start.2 = ((s8[5242880]{0:T(1024)(128)(4,1)}), s8[4194304]{0:T(1024)(128)(4,1)S(1)}, s32[]{:S(2)}) async-start(s8[5242880]{0:T(1024)(128)(4,1)} %bitcast.201), calls=%async_computation.16 | async-start | bytes 8388608
  264.3 6.0 %slice-start.3 = ((s8[5242880]{0:T(1024)(128)(4,1)}), s8[1048576]{0:T(1024)(128)(4,1)S(1)}, s32[]{:S(2)}) async-start(s8[5242880]{0:T(1024)(128)(4,1)} %bitcast.201), calls=%async_computation.17 | async-start | bytes 2097152
  281.8 26.5 %copy-start.6 = (f32[1024,512]{1,0:T(8,128)S(1)}, f32[1024,512]{1,0:T(8,128)}, u32[]{:S(2)}) copy-start(f32[1024,512]{1,0:T(8,128)} %get-tuple-element.21) | copy-start | bytes 6291460
  281.8 26.5 %copy-start.9 = (f32[1,512]{1,0:T(1,128)S(1)}, f32[1,512]{1,0:T(1,128)}, u32[]{:S(2)}) copy-start(f32[1,512]{1,0:T(1,128)} %param.9) | copy-start | bytes 6148
  282.5 27.5 %all-to-all-start.2 = ((f32[32,4,576]{2,1,0:T(4,128)}), f32[32,4,576]{2,1,0:T(4,128)S(1)}, u32[]{:S(2)}, u32[]{:S(2)}) async-start(f32[32,4,576]{2,1,0:T(4,128)} %broadcast_in_dim.20), calls=%async_computation.6 | async-start | bytes 655360 | tf_op jit(solution)/shard_map/all_to_all | solution.py:27
  310.6 11.2 %all-to-all-start.1 = ((f32[2,1,512]{2,1,0:T(1,128)}), f32[2,1,512]{2,1,0:T(1,128)S(1)}, u32[]{:S(2)}, u32[]{:S(2)}) async-start(f32[2,1,512]{2,1,0:T(1,128)} %broadcast_in_dim.18), calls=%async_computation.4 | async-start | bytes 8192 | tf_op jit(solution)/shard_map/all_to_all | solution.py:27
  321.8 60.4 %all-to-all-start = ((bf16[2,1152,512]{1,2,0:T(8,128)(2,1)}), bf16[2,1152,512]{1,2,0:T(8,128)(2,1)}, u32[]{:S(2)}, u32[]{:S(2)}) async-start(bf16[2,1152,512]{1,2,0:T(8,128)(2,1)} %bitcast.194), calls=%async_computation.3 | async-start | bytes 4718592 | tf_op jit(solution)/shard_map/all_to_all | solution.py:37
  326.8 86.1 %copy-start.1 = (bf16[1,2304,512]{2,1,0:T(8,128)(2,1)S(1)}, bf16[1,2304,512]{2,1,0:T(8,128)(2,1)}, u32[]{:S(2)}) copy-start(bf16[1,2304,512]{2,1,0:T(8,128)(2,1)} %param.8) | copy-start | bytes 7077892
Sparse Core Ops, SparseCore 0:
  9.7 41.0 all-gather.7
  57.5 48.5 all-gather.9
  139.1 15.8 reduce-scatter.4
  157.5 45.6 reduce-scatter.6
  205.4 38.6 all-gather.5
  261.0 47.1 reduce-scatter.8
  311.2 101.6 reduce-scatter.10
where the time goes:
time: 421 us; the launch traced here: 420 us
  waiting for transfers between devices  295 us (70%)
  matrix products  69.3 us (16%)
  starting transfers between devices  15.6 us (4%)
  between operations  14.4 us (3%)
  local copies, waits for them, and re-layouts  12.5 us (3%)
  other arithmetic  12.5 us (3%)
    all_to_all x1, waiting for transfers between devices, sent_and_summed(): lax.all_to_all(blocks, axis, split_axis=0, concat_axis=0, tiled=True)  54.2 us
    all_gather x1, waiting for transfers between devices, per_device(): sources = lax.all_gather(acts[None], 'layer', axis=0, tiled=True)  48.6 us
    reduce_scatter x1, waiting for transfers between devices, summed_rows_2(): return lax.psum_scatter(blocks, chips, scatter_dimension=0, tiled=True)[0]  48.1 us
    all_gather x1, waiting for transfers between devices, per_device(): rows = lax.all_gather(inputs[0], FEAT, axis=0, tiled=True)  42.8 us
    all_gather x1, waiting for transfers between devices, per_device(): lax.all_gather((errors / total_tokens).astype(jnp.bfloat16), FEAT, axis=0...  38.8 us
    reduce_scatter x1, waiting for transfers between devices, per_device(): lax.psum_scatter(terms.astype(jnp.bfloat16), 'grp', scatter_dimension=0,...  26.5 us
    dot_general x10, matrix products, decode_target(): jnp.dot(block[source], dec_weight[index], preferred_element_type=jnp.floa...  22.2 us
    dot_general x10, matrix products, per_device(): jnp.einsum('rf,rd->fd', sources[s], derr[:, t, :], preferred_element_type...  20.8 us
  transfers between devices with their start and end apart: 10, of which 8 were waited for; matrix products, arithmetic and copies ran while one was open for 9% of the time, Pallas kernels for 0%

commit v1 on v0

v1 whole, which is shorter than its diff:
```python
import jax
import jax.numpy as jnp
from jax import lax
from jax.experimental import pallas as pl
from jax.experimental.pallas import tpu as pltpu
from jax.sharding import Mesh
from jax.sharding import PartitionSpec as P

X, Y, C, Z, G = ("feat_0", "feat_1", "feat_2", "layer", "grp")
FEAT = (X, Y, C)
GRP_FEAT = (G, X, Y, C)
BF16, F32 = (jnp.bfloat16, jnp.float32)
VMEM = pl.BlockSpec(memory_space=pltpu.VMEM)
SMEM = pl.BlockSpec(memory_space=pltpu.SMEM)


def from_offset(x, axis, offset):
    size = lax.axis_size(axis)
    return lax.ppermute(x, axis, [((i + offset) % size, i) for i in range(size)])


def to_offset(x, axis, offset):
    return from_offset(x, axis, -offset)


def call(body, outs, args, scratch=(), flops=0, scalars=0, limit=56):
    moved = sum(a.size * a.dtype.itemsize for a in args)
    for shape, dtype in outs:
        count = 1
        for n in shape:
            count *= n
        moved += count * jnp.dtype(dtype).itemsize
    return pl.pallas_call(
        body,
        out_shape=[jax.ShapeDtypeStruct(s, d) for s, d in outs],
        in_specs=[SMEM] * scalars + [VMEM] * (len(args) - scalars),
        out_specs=[VMEM] * len(outs),
        scratch_shapes=list(scratch),
        cost_estimate=pl.CostEstimate(flops=flops, bytes_accessed=moved, transcendentals=0),
        compiler_params=pltpu.CompilerParams(vmem_limit_bytes=limit << 20),
    )(*args)


def lay_rows(parts, target):
    at = 0
    for part in parts:
        target[at : at + part.shape[0], :] = part[...]
        at += part.shape[0]


def encode(blocks, weight, bias):
    rows = sum(b.shape[0] for b in blocks)
    width, feats = weight.shape
    n = len(blocks)

    def body(*refs):
        parts, (w, b, joined, first, second, mask) = refs[:n], refs[n:]
        lay_rows(parts, joined)
        pre = jnp.dot(joined[...], w[...], preferred_element_type=F32) + b[...]
        acts = jnp.maximum(pre, 0.0).astype(BF16)
        first[...] = acts[: rows // 2]
        second[...] = acts[rows // 2 :]
        mask[...] = jnp.where(pre > 0, 1.0, 0.0).astype(BF16)

    half = ((rows // 2, feats), BF16)
    return call(
        body,
        [((rows, width), BF16), half, half, ((rows, feats), BF16)],
        [*blocks, weight, bias],
        flops=2 * rows * width * feats,
    )


def fresh(x, edge):
    lane = lax.broadcasted_iota(jnp.int32, x.shape, 1)
    return jnp.where(lane >= edge, x, jnp.zeros_like(x))


def nt(a, b):
    return lax.dot_general(a, b, (((1,), (1,)), ((), ())), preferred_element_type=F32)


def nn(a, b):
    return jnp.dot(a, b, preferred_element_type=F32)


def decode(here, sources, weight, block):
    half, feats = sources[0][0].shape
    rows = 2 * half
    d = block
    wide = 4 * d
    e = d % 128

    def body(here_ref, *refs):
        acts_in, (w, acts, keep, send) = refs[:8], refs[8:]
        for step in range(4):
            layer = lax.rem(here_ref[0] + step, 4)
            acts[layer, :half, :] = acts_in[2 * step][...]
            acts[layer, half:, :] = acts_in[2 * step + 1][...]
        for at, out in ((half, send), (0, keep)):
            a = [acts[s, at : at + half, :] for s in range(4)]
            out[:, : d - e] = nt(a[0], w[: d - e, :]).astype(BF16)
            part = nt(a[0], w[d - e : 2 * d, :]) + fresh(nt(a[1], w[4 * d - e : 5 * d, :]), e)
            out[:, d - e : 2 * d] = part.astype(BF16)
            part = (
                nt(a[0], w[2 * d : 3 * d - e, :])
                + nt(a[1], w[5 * d : 6 * d - e, :])
                + nt(a[2], w[7 * d : 8 * d - e, :])
            )
            out[:, 2 * d : 3 * d - e] = part.astype(BF16)
            part = (
                nt(a[0], w[3 * d - e : 4 * d, :])
                + nt(a[1], w[6 * d - e : 7 * d, :])
                + nt(a[2], w[8 * d - e : 9 * d, :])
                + fresh(nt(a[3], w[9 * d - e :, :]), e)
            )
            out[:, 3 * d - e :] = part.astype(BF16)

    return call(
        body,
        [((4, rows, feats), BF16), ((half, wide), BF16), ((half, wide), BF16)],
        [here, *[x for pair in sources for x in pair], weight],
        flops=20 * rows * feats * d,
        scalars=1,
    )


def feature_grads(here, blocks, weight, block):
    rows = sum(b.shape[0] for b in blocks)
    feats = weight.shape[1]
    d = block
    e = d % 128
    half = rows // 2
    n = len(blocks)

    def body(here_ref, *refs):
        parts, w, joined, outs, held = refs[:n], refs[n], refs[n + 1], refs[n + 2 : n + 10], refs[n + 10]
        lay_rows(parts, joined)

        def slot(layer):
            return lax.rem(layer + 4 - here_ref[0], 4)

        x = joined[...]
        held[slot(0)] = nn(x, w[: 4 * d, :]).astype(BF16)
        part = jnp.concatenate([fresh(x[:, d - e : d - e + 128], e), x[:, d - e + 128 :]], axis=1)
        held[slot(1)] = nn(part, w[4 * d - e : 7 * d, :]).astype(BF16)
        held[slot(2)] = nn(x[:, 2 * d :], w[7 * d : 9 * d, :]).astype(BF16)
        part = jnp.concatenate([fresh(x[:, 3 * d - e : 3 * d - e + 128], e), x[:, 3 * d - e + 128 :]], axis=1)
        held[slot(3)] = nn(part, w[9 * d - e :, :]).astype(BF16)
        for step in range(4):
            outs[2 * step][...] = held[step, :half, :]
            outs[2 * step + 1][...] = held[step, half:, :]

    res = call(
        body,
        [((rows, 4 * d), BF16)] + [((half, feats), BF16)] * 8,
        [here, *blocks, weight],
        scratch=[pltpu.VMEM((4, rows, feats), BF16)],
        flops=20 * rows * feats * d,
        scalars=1,
    )
    return res[0], res[1:]


def decoder_terms(acts, errors, block):
    _, rows, feats = acts[0].shape
    d = block
    e = d % 128
    n = len(acts)

    def body(*refs):
        a, x, out, turned = refs[:n], refs[n : 2 * n], refs[2 * n], refs[2 * n + 1]
        for k in range(n):
            turned[:, k * rows : (k + 1) * rows] = x[k][...].T
        at = 0
        for s in range(4):
            both = jnp.concatenate([a[k][s] for k in range(n)], axis=0)
            for t in range(s, 4):
                out[at : at + d, :] = nn(turned[t * d : (t + 1) * d, :], both).astype(BF16)
                at += d

    return call(
        body,
        [((10 * d, feats), BF16)],
        [*acts, *errors],
        scratch=[pltpu.VMEM((4 * d, n * rows), BF16)],
        flops=20 * n * rows * feats * d,
    )[0]


def gather_rows(block):
    half = block.shape[0] // 2
    x1 = from_offset(block, X, 1)
    y1 = from_offset(block, Y, 1)
    y3 = from_offset(block, Y, -1)
    near = jnp.concatenate([block, x1, y1, y3], axis=0)
    near_core = from_offset(near, C, 1)
    xy1 = from_offset(y1, X, 1)
    xy3 = from_offset(x1, Y, -1)
    y2 = from_offset(y1, Y, 1)
    xy2a = from_offset(xy1[:half], Y, 1)
    xy2b = from_offset(xy3[half:], Y, -1)
    far = jnp.concatenate([xy1, xy3, y2, xy2a, xy2b], axis=0)
    far_core = from_offset(far, C, 1)
    return [near, near_core], [far, far_core]


def sum_rows(near, far):
    rows = near[0].shape[0] // 4
    half = rows // 2
    near_in = from_offset(near[1], C, 1)
    far_in = from_offset(far[1], C, 1)

    def taken(pair, arrived, k):
        cut = slice(k * rows, (k + 1) * rows)
        return pair[cut].astype(F32) + arrived[cut].astype(F32)

    q00, q10, q01, q03 = [taken(near[0], near_in, k) for k in range(4)]
    q11, q13, q02, q12 = [taken(far[0], far_in, k) for k in range(4)]
    r03 = to_offset(q03.astype(BF16), Y, -1)
    a = to_offset(q12[:half].astype(BF16), Y, 1).astype(F32)
    b = to_offset(q12[half:].astype(BF16), Y, -1).astype(F32)
    r02 = to_offset(q02.astype(BF16), Y, 1)
    q11 = jnp.concatenate([q11[:half] + a, q11[half:]], axis=0)
    q13 = jnp.concatenate([q13[:half], q13[half:] + b], axis=0)
    r11 = to_offset(q11.astype(BF16), X, 1)
    r13 = to_offset(q13.astype(BF16), Y, -1)
    q01 = q01 + r11.astype(F32) + r02.astype(F32)
    q10 = q10 + r13.astype(F32)
    r01 = to_offset(q01.astype(BF16), Y, 1)
    r10 = to_offset(q10.astype(BF16), X, 1)
    return q00 + r03.astype(F32) + r01.astype(F32) + r10.astype(F32)


def gather_layers(first, second):
    a1 = from_offset(first, Z, 1)
    b3 = from_offset(second, Z, -1)
    b1 = from_offset(second, Z, 1)
    a3 = from_offset(first, Z, -1)
    a2 = from_offset(a1, Z, 1)
    b2 = from_offset(b3, Z, -1)
    return [(first, second), (a1, b1), (a2, b2), (a3, b3)]


def sum_layers(parts):
    a0, b0, a1, b1, a2, b2, a3, b3 = parts
    a2 = to_offset(a2, Z, 1)
    b2 = to_offset(b2, Z, -1)
    b1 = to_offset(b1, Z, 1)
    a3 = to_offset(a3, Z, -1)
    a1 = to_offset((a1.astype(F32) + a2.astype(F32)).astype(BF16), Z, 1)
    b3 = to_offset((b3.astype(F32) + b2.astype(F32)).astype(BF16), Z, -1)
    first = a0.astype(F32) + a1.astype(F32) + a3.astype(F32)
    second = b0.astype(F32) + b1.astype(F32) + b3.astype(F32)
    return jnp.concatenate([first, second], axis=0)


def exchanged(x):
    own = lax.axis_index(G)
    half = x.shape[0] // 2
    sent = lax.dynamic_slice_in_dim(x, (1 - own) * half, half, 0)
    kept = lax.dynamic_slice_in_dim(x, own * half, half, 0)
    arrived = from_offset(sent, G, 1)
    return (kept.astype(F32) + arrived.astype(F32)).astype(x.dtype)


def per_device(inputs, targets, enc_weight, enc_bias, dec_weight, dec_bias):
    layers, d = dec_bias.shape
    here = lax.axis_index(Z).astype(jnp.int32)[None]
    tok_dev = inputs.shape[1]
    total_tokens = tok_dev * lax.axis_size(FEAT) * lax.axis_size(G)
    feats = dec_weight.shape[1]
    decoder = dec_weight.transpose(0, 2, 1).reshape(-1, feats)
    wanted = targets.astype(F32).reshape(tok_dev, -1) - dec_bias.reshape(1, -1)

    chunks = gather_rows(inputs[0])
    rows, masks, acts, partial = [], [], [], []
    for chunk in chunks:
        joined, first, second, mask = encode(chunk, enc_weight[0], enc_bias)
        rows.append(joined)
        masks.append(mask)
        a, keep, send = decode(here, gather_layers(first, second), decoder, d)
        acts.append(a)
        partial.append((keep, send))
    errors = sum_rows(*partial) - wanted
    dec_bias_grad = lax.psum(jnp.sum(errors, axis=0), GRP_FEAT) / total_tokens
    scaled = (errors / total_tokens).astype(BF16)

    derr, dpre = [], []
    for chunk, mask in zip(gather_rows(scaled), masks):
        joined, parts = feature_grads(here, chunk, decoder, d)
        derr.append(joined)
        dacts = sum_layers(parts)
        dpre.append(jnp.where(mask > 0, dacts, jnp.zeros_like(dacts)))
    dec_grad = exchanged(decoder_terms(acts, derr, d))
    enc_bias_grad = sum(jnp.sum(x, axis=0) for x in dpre)
    enc_bias_grad = enc_bias_grad + from_offset(enc_bias_grad, G, 1)
    enc_grad = sum(
        jnp.einsum("rd,rf->df", r, x.astype(BF16), preferred_element_type=F32) for r, x in zip(rows, dpre)
    )
    enc_grad = exchanged(enc_grad.astype(BF16))
    return (
        enc_grad[None],
        enc_bias_grad[None],
        dec_grad.reshape(-1, d, feats).transpose(0, 2, 1),
        dec_bias_grad.reshape(layers, d),
    )


def solution(mesh):
    finer = Mesh(
        mesh.devices.reshape(mesh.shape["grp"], mesh.shape["layer"], 2, 4, 2),
        (G, Z, X, Y, C),
    )
    return jax.shard_map(
        per_device,
        mesh=finer,
        in_specs=(
            P(Z, GRP_FEAT, None),
            P(GRP_FEAT, None, Z),
            P(Z, None, FEAT),
            P(Z, FEAT),
            P(None, FEAT, Z),
            P(None, Z),
        ),
        out_specs=(P(Z, G, FEAT), P(Z, FEAT), P(G, FEAT, Z), P(None, Z)),
        check_vma=False,
    )
```

time: 421 us -> 465 us (1.10); the launches traced: 420 us -> 456 us
  blocking collectives: 0 us -> 187 us
  waiting for transfers between devices: 295 us -> 109 us
  matrix products: 69.3 us -> 2.86 us
  Pallas kernels: 0 us -> 58 us
  starting transfers between devices: 15.6 us -> 69.3 us
  between operations: 14.4 us -> 1.6 us
    psum x0 -> x1, blocking collectives: none -> 187 us  [per_device(): dec_bias_grad = lax.psum(jnp.sum(errors, axis=0), GRP_FEAT) / total_tokens]
    all_gather x3 -> x0, waiting for transfers between devices: 130 us -> none  [the longest x1 48.6 us: per_device(): sources = lax.all_gather(acts[None], 'layer', axis=0, tiled=True)]
    reduce_scatter x4 -> x0, waiting for transfers between devices: 110 us -> none  [the longest x1 48.1 us: summed_rows_2(): return lax.psum_scatter(blocks, chips, scatter_dimension=0, tiled=True)[0]]
    ppermute x0 -> x57, waiting for transfers between devices: none -> 109 us  [from_offset(): lax.ppermute(x, axis, [((i + offset) % size, i) for i in range(size)])]
    ppermute x0 -> x57, starting transfers between devices: none -> 69.3 us  [from_offset(): lax.ppermute(x, axis, [((i + offset) % size, i) for i in range(size)])]
    dot_general x32 -> x2, matrix products: 69.3 us -> 2.86 us  [per_device(): jnp.einsum('rd,rf->df', r, x.astype(BF16), preferred_element_type=F32)]
    pallas_call x0 -> x7, Pallas kernels: none -> 58 us  [call(): pl.pallas_call(body, out_shape=[jax.ShapeDtypeStruct(s, d) for s, d in ou...]
    all_to_all x3 -> x0, waiting for transfers between devices: 54.2 us -> none  [the longest x1 54.2 us: sent_and_summed(): lax.all_to_all(blocks, axis, split_axis=0, concat_axis=0, tiled=True)]
  transfers between devices with their start and end apart: 10 -> 57, of which waited for: 8 -> 32; matrix products, arithmetic and copies ran while one was open for 9% -> 4% of each run, Pallas kernels for 0% -> 13%
where the time goes in v1:
time: 465 us; the launch traced here: 456 us
  blocking collectives  187 us (40%)
  waiting for transfers between devices  109 us (23%)
  starting transfers between devices  69.3 us (15%)
  Pallas kernels  58 us (12%)
  other arithmetic  15.5 us (3%)
  local copies, waits for them, and re-layouts  12.7 us (3%)
    psum x1, blocking collectives, per_device(): dec_bias_grad = lax.psum(jnp.sum(errors, axis=0), GRP_FEAT) / total_tokens  187 us
    ppermute x57, waiting for transfers between devices, from_offset(): lax.ppermute(x, axis, [((i + offset) % size, i) for i in range(size)])  109 us
    ppermute x57, starting transfers between devices, from_offset(): lax.ppermute(x, axis, [((i + offset) % size, i) for i in range(size)])  69.3 us
    pallas_call x7, Pallas kernels, call(): pl.pallas_call(body, out_shape=[jax.ShapeDtypeStruct(s, d) for s, d in ou...  58 us
  transfers between devices with their start and end apart: 57, of which 32 were waited for; matrix products, arithmetic and copies ran while one was open for 4% of the time, Pallas kernels for 13%

profile of v1, /device:TPU:0, one launch (start us, length us, event | category | flops | bytes accessed | tf_op | source)
XLA Modules:
  0.0 455.8 jit_solution(3258786996750991742)
XLA Ops:
  0.6 3.2 collective-permute-start.1
  3.8 1.5 collective-permute-start
  5.3 5.1 %collective-permute-done.1 = bf16[64,2304]{1,0:T(8,128)(2,1)S(1)} collective-permute-done((bf16[64,2304]{1,0:T(8,128)(2,1)}, bf16[64,2304]{1,0:T(8,128)(2,1)S(1)}, u32[]{:S(2)}, u32[]{:S(2)}) %collective-permute-start.1) | collective-permute-done | bytes 294944 | tf_op jit(solution)/shard_map/ppermute | solution.py:19
  10.4 1.5 collective-permute-start.12
  13.0 3.2 collective-permute-start.14
  16.2 2.6 collective-permute-done.12
  18.8 3.1 collective-permute-start.15
  22.1 2.5 collective-permute-done.15
  24.6 3.8 collective-permute-done.16
  28.6 2.7 collective-permute-done.17.refs_1_
  32.3 5.3 %shard_map.95 = (bf16[512,2304]{1,0:T(8,128)(2,1)}, bf16[256,512]{1,0:T(8,128)(2,1)}, bf16[256,512]{1,0:T(8,128)(2,1)}, bf16[512,512]{1,0:T(8,128)(2,1)}) custom-call(bf16[256,2304]{1,0:T(8,128)(2,1)} %copy-done.10, bf16[256,2304]{1,0:T(8,128)(2,1)} %copy-done.15, bf16[2304,512]{1,0:T(8,128)(2,1)} %bitcast.14, f32[1,512]{1,0:T(1,128)} %refs_3_.3), custom_call_target="tpu_custom_call" | custom-call | flops 1207959552 | bytes 8128512 | tf_op jit(solution)/shard_map/pallas_call | solution.py:33
  37.7 4.0 collective-permute-start.18
  41.7 3.2 collective-permute-start.19
  45.0 3.7 collective-permute-done.18.refs_2_
  48.7 3.6 collective-permute-start.20
  54.3 3.6 collective-permute-done.23.refs_6_
  59.0 3.5 collective-permute-done.22.refs_5_
  62.5 8.6 %shard_map.96 = (bf16[4,512,512]{2,1,0:T(8,128)(2,1)}, bf16[256,2304]{1,0:T(8,128)(2,1)}, bf16[256,2304]{1,0:T(8,128)(2,1)}) custom-call(s32[1]{0:T(128)} %bitcast.2.here_ref, bf16[256,512]{1,0:T(8,128)(2,1)} %get-tuple-element.42.refs_0_, bf16[256,512]{1,0:T(8,128)(2,1)} %get-tuple-element.43.refs_1_, bf16[256,512]{1,0:T(8,128)(2,1)} %copy-done.30, ...), custom_call_target="tpu_custom_call" | custom-call | flops 3019898880 | bytes 12451844 | tf_op jit(solution)/shard_map/pallas_call | solution.py:33
  72.3 5.3 %shard_map.93 = (bf16[512,2304]{1,0:T(8,128)(2,1)}, bf16[256,512]{1,0:T(8,128)(2,1)}, bf16[256,512]{1,0:T(8,128)(2,1)}, bf16[512,512]{1,0:T(8,128)(2,1)}) custom-call(bf16[256,2304]{1,0:T(8,128)(2,1)} %copy-done.5, bf16[256,2304]{1,0:T(8,128)(2,1)} %copy-done.14, bf16[2304,512]{1,0:T(8,128)(2,1)} %bitcast.15, f32[1,512]{1,0:T(1,128)} %refs_3_.3), custom_call_target="tpu_custom_call" | custom-call | flops 1207959552 | bytes 8128512 | tf_op jit(solution)/shard_map/pallas_call | solution.py:33
  77.9 1.7 collective-permute-start.7
  79.6 1.9 collective-permute-start.5
  82.0 4.9 %collective-permute-done.4.refs_2_ = bf16[256,512]{1,0:T(8,128)(2,1)S(1)} collective-permute-done((bf16[256,512]{1,0:T(8,128)(2,1)}, bf16[256,512]{1,0:T(8,128)(2,1)S(1)}, u32[]{:S(2)}, u32[]{:S(2)}) %collective-permute-start.4) | collective-permute-done | bytes 262176 | tf_op jit(solution)/shard_map/ppermute | solution.py:19
  86.9 1.5 collective-permute-start.6
  89.8 2.7 collective-permute-done.5.refs_3_
  92.5 1.5 collective-permute-done.9.refs_6_
  94.1 3.7 collective-permute-done.6.refs_4_
  99.7 8.6 %shard_map.94 = (bf16[4,512,512]{2,1,0:T(8,128)(2,1)}, bf16[256,2304]{1,0:T(8,128)(2,1)}, bf16[256,2304]{1,0:T(8,128)(2,1)}) custom-call(s32[1]{0:T(128)} %bitcast.2.here_ref, bf16[256,512]{1,0:T(8,128)(2,1)} %get-tuple-element.38.refs_0_, bf16[256,512]{1,0:T(8,128)(2,1)} %get-tuple-element.39.refs_1_, bf16[256,512]{1,0:T(8,128)(2,1)} %copy-done.31, ...), custom_call_target="tpu_custom_call" | custom-call | flops 3019898880 | bytes 12451844 | tf_op jit(solution)/shard_map/pallas_call | solution.py:33
  108.6 3.3 collective-permute-start.30
  111.9 10.3 %collective-permute-done.25 = bf16[32,2304]{1,0:T(8,128)(2,1)S(1)} collective-permute-done((bf16[32,2304]{1,0:T(8,128)(2,1)S(1)}, bf16[32,2304]{1,0:T(8,128)(2,1)S(1)}, u32[]{:S(2)}, u32[]{:S(2)}) %collective-permute-start.25) | collective-permute-done | bytes 147488 | tf_op jit(solution)/shard_map/ppermute | solution.py:19
  122.2 1.6 collective-permute-start.26
  123.8 7.1 %collective-permute-done.26 = bf16[64,2304]{1,0:T(8,128)(2,1)S(1)} collective-permute-done((bf16[64,2304]{1,0:T(8,128)(2,1)S(1)}, bf16[64,2304]{1,0:T(8,128)(2,1)S(1)}, u32[]{:S(2)}, u32[]{:S(2)}) %collective-permute-start.26) | collective-permute-done | bytes 294944 | tf_op jit(solution)/shard_map/ppermute | solution.py:19
  132.1 1.5 collective-permute-start.31
  133.6 3.2 collective-permute-start.11
  137.1 3.0 collective-permute-done.31
  140.2 2.4 collective-permute-done.28
  142.6 1.4 fusion.17
  144.0 3.0 collective-permute-start.33
  147.6 3.7 collective-permute-done.33
  151.8 4.9 %collective-permute-done.32 = bf16[64,2304]{1,0:T(8,128)(2,1)S(1)} collective-permute-done((bf16[64,2304]{1,0:T(8,128)(2,1)S(1)}, bf16[64,2304]{1,0:T(8,128)(2,1)S(1)}, u32[]{:S(2)}, u32[]{:S(2)}) %collective-permute-start.32) | collective-permute-done | bytes 294944 | tf_op jit(solution)/shard_map/ppermute | solution.py:19
  157.4 2.9 collective-permute-start.44
  160.2 1.6 collective-permute-start.45
  161.8 2.9 collective-permute-done.43
  165.0 2.5 collective-permute-done.44
  167.6 2.7 collective-permute-done.45
  172.6 8.8 %shard_map.97 = (bf16[512,2304]{1,0:T(8,128)(2,1)}, bf16[256,512]{1,0:T(8,128)(2,1)}, bf16[256,512]{1,0:T(8,128)(2,1)}, bf16[256,512]{1,0:T(8,128)(2,1)}, bf16[2...) custom-call(s32[1]{0:T(128)} %bitcast.2.here_ref, ...), custom_call_target="tpu_custom_call" | custom-call | flops 3019898880 | bytes 12713988 | tf_op jit(solution)/shard_map/pallas_call | solution.py:33
  184.0 2.7 collective-permute-start.38
  186.7 4.1 collective-permute-done.40
  191.8 2.3 collective-permute-start.41
  196.3 8.9 %shard_map.98 = (bf16[512,2304]{1,0:T(8,128)(2,1)}, bf16[256,512]{1,0:T(8,128)(2,1)}, bf16[256,512]{1,0:T(8,128)(2,1)}, bf16[256,512]{1,0:T(8,128)(2,1)}, bf16[2...) custom-call(s32[1]{0:T(128)} %bitcast.2.here_ref, ...), custom_call_target="tpu_custom_call" | custom-call | flops 3019898880 | bytes 12713988 | tf_op jit(solution)/shard_map/pallas_call | solution.py:33
  205.2 3.2 collective-permute-start.52
  208.4 12.4 %shard_map.99 = bf16[5760,512]{1,0:T(8,128)(2,1)} custom-call(bf16[4,512,512]{2,1,0:T(8,128)(2,1)} %get-tuple-element.64.refs_0_, bf16[4,512,512]{2,1,0:T(8,128)(2,1)} %get-tuple-element.65.refs_1_, bf16[512,2304]{1,0:T(8,128)(2,1)} %get-tuple-element.66.refs_2_, bf16[512,2304]{1,0:T(8,128)(2,1)} %get-tuple-element.67.refs_3_), custom_call_target="tpu_custom_call" | custom-call | flops 6039797760 | bytes 14811136 | tf_op jit(solution)/shard_map/pallas_call | solution.py:33
  220.8 3.7 constant_dynamic-slice_fusion
  225.5 2.9 collective-permute-start.50
  228.4 9.4 %collective-permute-done.48 = bf16[256,512]{1,0:T(8,128)(2,1)S(1)} collective-permute-done((bf16[256,512]{1,0:T(8,128)(2,1)S(1)}, bf16[256,512]{1,0:T(8,128)(2,1)S(1)}, u32[]{:S(2)}, u32[]{:S(2)}) %collective-permute-start.48) | collective-permute-done | bytes 262176 | tf_op jit(solution)/shard_map/ppermute | solution.py:19
  237.9 2.8 collective-permute-start.56
  240.7 2.0 collective-permute-start.49
  244.3 4.0 collective-permute-done.49
  248.5 1.4 fusion.2
  250.4 1.4 fusion
  253.7 186.5 %psum.7 = f32[2304]{0:T(1024)S(1)} all-reduce(f32[2304]{0:T(1024)S(1)} %get-tuple-element.68), channel_id=1, replica_groups=mesh['grp'=2,'layer'=4,'feat_0'=2,'feat_1'=4,'feat_2'=2] {'grp','feat_0'..., use_global_device_ids=true, to_apply=%region_3.4 | all-reduce | flops 2304 | bytes 18432 | tf_op jit(solution)/shard_map/psum | solution.py:286
  440.2 1.3 fusion.6
  442.8 4.4 collective-permute-done.55
  447.8 2.6 fusion.1
  450.4 5.2 %add_convert_fusion = bf16[2880,512]{1,0:T(8,128)(2,1)} fusion(bf16[2880,512]{1,0:T(8,128)(2,1)} %collective-permute-done.56, bf16[5760,512]{1,0:T(8,128)(2,1)} %shard_map.99, s32[]{:T(128)S(6)} %select_n.23), kind=kLoop, calls=%fused_computation | loop fusion | flops 5898240 | bytes 8847364 | tf_op jit(solution)/shard_map/convert_element_type | solution.py:264
  (189 shorter events, 29.4 us)
Async XLA Ops:
  0.6 9.7 %collective-permute-start.1 = (bf16[64,2304]{1,0:T(8,128)(2,1)}, bf16[64,2304]{1,0:T(8,128)(2,1)S(1)}, u32[]{:S(2)}, u32[]{:S(2)}) collective-permute-start(bf16[64,2304]{1,0:T(8,128)(2,1)} %bitcast.17), channel_id=1, source_target_pairs={{2,0},{4,2},{6,4},{0,6},{3,1},{5,3},{7,5},{1,7},{10,8},{12,10},{14... | collective-permute-start | bytes 884744 | tf_op jit(solution)/shard_map/ppermute | solution.py:19
  3.8 9.2 %collective-permute-start = (bf16[64,2304]{1,0:T(8,128)(2,1)}, bf16[64,2304]{1,0:T(8,128)(2,1)S(1)}, u32[]{:S(2)}, u32[]{:S(2)}) collective-permute-start(bf16[64,2304]{1,0:T(8,128)(2,1)} %bitcast.18), channel_id=1, source_target_pairs={{8,0},{0,8},{9,1},{1,9},{10,2},{2,10},{11,3},{3,11},{12,4},{4,12},... | collective-permute-start | bytes 884744 | tf_op jit(solution)/shard_map/ppermute | solution.py:19
  10.4 8.4 %collective-permute-start.12 = (bf16[64,2304]{1,0:T(8,128)(2,1)S(1)}, bf16[64,2304]{1,0:T(8,128)(2,1)S(1)}, u32[]{:S(2)}, u32[]{:S(2)}) collective-permute-start(bf16[64,2304]{1,0:T(8,128)(2,1)S(1)} %collective-permute-done.1), channel_id=1, source_target_pairs={{8,0},{0,8},{9,1},{1,9},{10,2},{2,10},{11,3},{3,11},{12,4},{4,12},... | collective-permute-start | bytes 884744 | tf_op jit(solution)/shard_map/ppermute | solution.py:19
  12.9 9.0 %collective-permute-start.13 = (bf16[64,2304]{1,0:T(8,128)(2,1)S(1)}, bf16[64,2304]{1,0:T(8,128)(2,1)S(1)}, u32[]{:S(2)}, u32[]{:S(2)}) collective-permute-start(bf16[64,2304]{1,0:T(8,128)(2,1)S(1)} %collective-permute-done), channel_id=1, source_target_pairs={{6,0},{0,2},{2,4},{4,6},{7,1},{1,3},{3,5},{5,7},{14,8},{8,10},{10,... | collective-permute-start | bytes 884744 | tf_op jit(solution)/shard_map/ppermute | solution.py:19
  13.0 9.1 %collective-permute-start.14 = (bf16[64,2304]{1,0:T(8,128)(2,1)S(1)}, bf16[64,2304]{1,0:T(8,128)(2,1)S(1)}, u32[]{:S(2)}, u32[]{:S(2)}) collective-permute-start(bf16[64,2304]{1,0:T(8,128)(2,1)S(1)} %collective-permute-done.1), channel_id=1, source_target_pairs={{2,0},{4,2},{6,4},{0,6},{3,1},{5,3},{7,5},{1,7},{10,8},{12,10},{14... | collective-permute-start | bytes 884744 | tf_op jit(solution)/shard_map/ppermute | solution.py:19
  18.8 5.8 %collective-permute-start.15 = (bf16[32,2304]{1,0:T(8,128)(2,1)S(1)}, bf16[32,2304]{1,0:T(8,128)(2,1)S(1)}, u32[]{:S(2)}, u32[]{:S(2)}) collective-permute-start(bf16[32,2304]{1,0:T(8,128)(2,1)S(1)} %slice.111), channel_id=1, source_target_pairs={{2,0},{4,2},{6,4},{0,6},{3,1},{5,3},{7,5},{1,7},{10,8},{12,10},{14... | collective-permute-start | bytes 442376 | tf_op jit(solution)/shard_map/ppermute | solution.py:19
  22.0 6.4 %collective-permute-start.16 = (bf16[32,2304]{1,0:T(8,128)(2,1)S(1)}, bf16[32,2304]{1,0:T(8,128)(2,1)S(1)}, u32[]{:S(2)}, u32[]{:S(2)}) collective-permute-start(bf16[32,2304]{1,0:T(8,128)(2,1)S(1)} %slice.112), channel_id=1, source_target_pairs={{6,0},{0,2},{2,4},{4,6},{7,1},{1,3},{3,5},{5,7},{14,8},{8,10},{10,... | collective-permute-start | bytes 442376 | tf_op jit(solution)/shard_map/ppermute | solution.py:19
  28.4 2.9 collective-permute-start.17
  28.5 23.8 %collective-permute-start.2 = (bf16[64,2304]{1,0:T(8,128)(2,1)S(1)}, bf16[64,2304]{1,0:T(8,128)(2,1)S(1)}, u32[]{:S(2)}, u32[]{:S(2)}) collective-permute-start(bf16[64,2304]{1,0:T(8,128)(2,1)S(1)} %bitcast.19), channel_id=1, source_target_pairs={{6,0},{0,2},{2,4},{4,6},{7,1},{1,3},{3,5},{5,7},{14,8},{8,10},{10,... | collective-permute-start | bytes 884744 | tf_op jit(solution)/shard_map/ppermute | solution.py:19
  37.7 11.0 %collective-permute-start.18 = (bf16[256,512]{1,0:T(8,128)(2,1)}, bf16[256,512]{1,0:T(8,128)(2,1)S(1)}, u32[]{:S(2)}, u32[]{:S(2)}) collective-permute-start(bf16[256,512]{1,0:T(8,128)(2,1)} %get-tuple-element.42.refs_0_), channel_id=1, source_target_pairs={{16,0},{32,16},{48,32},{0,48},{17,1},{33,17},{49,33},{1,49},{18,2}... | collective-permute-start | bytes 786440 | tf_op jit(solution)/shard_map/ppermute | solution.py:19
  41.7 10.6 %collective-permute-start.21 = (bf16[256,512]{1,0:T(8,128)(2,1)}, bf16[256,512]{1,0:T(8,128)(2,1)S(1)}, u32[]{:S(2)}, u32[]{:S(2)}) collective-permute-start(bf16[256,512]{1,0:T(8,128)(2,1)} %get-tuple-element.43.refs_1_), channel_id=1, source_target_pairs={{48,0},{0,16},{16,32},{32,48},{49,1},{1,17},{17,33},{33,49},{50,2}... | collective-permute-start | bytes 786440 | tf_op jit(solution)/shard_map/ppermute | solution.py:19
  41.7 12.6 %collective-permute-start.19 = (bf16[256,512]{1,0:T(8,128)(2,1)}, bf16[256,512]{1,0:T(8,128)(2,1)S(1)}, u32[]{:S(2)}, u32[]{:S(2)}) collective-permute-start(bf16[256,512]{1,0:T(8,128)(2,1)} %get-tuple-element.43.refs_1_), channel_id=1, source_target_pairs={{16,0},{32,16},{48,32},{0,48},{17,1},{33,17},{49,33},{1,49},{18,2}... | collective-permute-start | bytes 786440 | tf_op jit(solution)/shard_map/ppermute | solution.py:19
  45.0 13.0 %collective-permute-start.23 = (bf16[256,512]{1,0:T(8,128)(2,1)}, bf16[256,512]{1,0:T(8,128)(2,1)S(1)}, u32[]{:S(2)}, u32[]{:S(2)}) collective-permute-start(bf16[256,512]{1,0:T(8,128)(2,1)} %get-tuple-element.42.refs_0_), channel_id=1, source_target_pairs={{48,0},{0,16},{16,32},{32,48},{49,1},{1,17},{17,33},{33,49},{50,2}... | collective-permute-start | bytes 786440 | tf_op jit(solution)/shard_map/ppermute | solution.py:19
  48.7 10.3 %collective-permute-start.20 = (bf16[256,512]{1,0:T(8,128)(2,1)S(1)}, bf16[256,512]{1,0:T(8,128)(2,1)}, u32[]{:S(2)}, u32[]{:S(2)}) collective-permute-start(bf16[256,512]{1,0:T(8,128)(2,1)S(1)} %collective-permute-done.18.refs_2_), channel_id=1, source_target_pairs={{16,0},{32,16},{48,32},{0,48},{17,1},{33,17},{49,33},{1,49},{18,2}... | collective-permute-start | bytes 786440 | tf_op jit(solution)/shard_map/ppermute | solution.py:19
  52.3 10.2 %collective-permute-start.22 = (bf16[256,512]{1,0:T(8,128)(2,1)S(1)}, bf16[256,512]{1,0:T(8,128)(2,1)}, u32[]{:S(2)}, u32[]{:S(2)}) collective-permute-start(bf16[256,512]{1,0:T(8,128)(2,1)S(1)} %collective-permute-done.21.refs_7_), channel_id=1, source_target_pairs={{48,0},{0,16},{16,32},{32,48},{49,1},{1,17},{17,33},{33,49},{50,2}... | collective-permute-start | bytes 786440 | tf_op jit(solution)/shard_map/ppermute | solution.py:19
  52.4 18.7 %copy-start.5 = (bf16[256,2304]{1,0:T(8,128)(2,1)}, bf16[256,2304]{1,0:T(8,128)(2,1)S(1)}, u32[]{:S(2)}) copy-start(bf16[256,2304]{1,0:T(8,128)(2,1)S(1)} %pad_maximum_fusion.refs_0_) | copy-start | bytes 3538948
  52.4 18.8 %collective-permute-start.3 = (bf16[256,2304]{1,0:T(8,128)(2,1)S(1)}, bf16[256,2304]{1,0:T(8,128)(2,1)S(1)}, u32[]{:S(2)}, u32[]{:S(2)}) collective-permute-start(bf16[256,2304]{1,0:T(8,128)(2,1)S(1)} %pad_maximum_fusion.refs_0_), channel_id=1, source_target_pairs={{1,0},{0,1},{3,2},{2,3},{5,4},{4,5},{7,6},{6,7},{9,8},{8,9},{11,10... | collective-permute-start | bytes 3538952 | tf_op jit(solution)/shard_map/ppermute | solution.py:19
  71.2 17.8 %copy-start.13 = (bf16[256,2304]{1,0:T(8,128)(2,1)S(1)}, bf16[256,2304]{1,0:T(8,128)(2,1)}, u32[]{:S(2)}) copy-start(bf16[256,2304]{1,0:T(8,128)(2,1)} %get-tuple-element.44) | copy-start | bytes 3538948
  71.2 17.8 %collective-permute-start.24 = (bf16[256,2304]{1,0:T(8,128)(2,1)}, bf16[256,2304]{1,0:T(8,128)(2,1)S(1)}, u32[]{:S(2)}, u32[]{:S(2)}) collective-permute-start(bf16[256,2304]{1,0:T(8,128)(2,1)} %get-tuple-element.45), channel_id=1, source_target_pairs={{1,0},{0,1},{3,2},{2,3},{5,4},{4,5},{7,6},{6,7},{9,8},{8,9},{11,10... | collective-permute-start | bytes 3538952 | tf_op jit(solution)/shard_map/ppermute | solution.py:19
  77.6 9.3 %collective-permute-start.4 = (bf16[256,512]{1,0:T(8,128)(2,1)}, bf16[256,512]{1,0:T(8,128)(2,1)S(1)}, u32[]{:S(2)}, u32[]{:S(2)}) collective-permute-start(bf16[256,512]{1,0:T(8,128)(2,1)} %get-tuple-element.38.refs_0_), channel_id=1, source_target_pairs={{16,0},{32,16},{48,32},{0,48},{17,1},{33,17},{49,33},{1,49},{18,2}... | collective-permute-start | bytes 786440 | tf_op jit(solution)/shard_map/ppermute | solution.py:19
  77.9 10.6 %collective-permute-start.7 = (bf16[256,512]{1,0:T(8,128)(2,1)}, bf16[256,512]{1,0:T(8,128)(2,1)S(1)}, u32[]{:S(2)}, u32[]{:S(2)}) collective-permute-start(bf16[256,512]{1,0:T(8,128)(2,1)} %get-tuple-element.39.refs_1_), channel_id=1, source_target_pairs={{48,0},{0,16},{16,32},{32,48},{49,1},{1,17},{17,33},{33,49},{50,2}... | collective-permute-start | bytes 786440 | tf_op jit(solution)/shard_map/ppermute | solution.py:19
  79.6 12.9 %collective-permute-start.5 = (bf16[256,512]{1,0:T(8,128)(2,1)}, bf16[256,512]{1,0:T(8,128)(2,1)S(1)}, u32[]{:S(2)}, u32[]{:S(2)}) collective-permute-start(bf16[256,512]{1,0:T(8,128)(2,1)} %get-tuple-element.39.refs_1_), channel_id=1, source_target_pairs={{16,0},{32,16},{48,32},{0,48},{17,1},{33,17},{49,33},{1,49},{18,2}... | collective-permute-start | bytes 786440 | tf_op jit(solution)/shard_map/ppermute | solution.py:19
  81.5 12.6 %collective-permute-start.9 = (bf16[256,512]{1,0:T(8,128)(2,1)}, bf16[256,512]{1,0:T(8,128)(2,1)S(1)}, u32[]{:S(2)}, u32[]{:S(2)}) collective-permute-start(bf16[256,512]{1,0:T(8,128)(2,1)} %get-tuple-element.38.refs_0_), channel_id=1, source_target_pairs={{48,0},{0,16},{16,32},{32,48},{49,1},{1,17},{17,33},{33,49},{50,2}... | collective-permute-start | bytes 786440 | tf_op jit(solution)/shard_map/ppermute | solution.py:19
  86.9 10.8 %collective-permute-start.6 = (bf16[256,512]{1,0:T(8,128)(2,1)S(1)}, bf16[256,512]{1,0:T(8,128)(2,1)S(1)}, u32[]{:S(2)}, u32[]{:S(2)}) collective-permute-start(bf16[256,512]{1,0:T(8,128)(2,1)S(1)} %collective-permute-done.4.refs_2_), channel_id=1, source_target_pairs={{16,0},{32,16},{48,32},{0,48},{17,1},{33,17},{49,33},{1,49},{18,2}... | collective-permute-start | bytes 786440 | tf_op jit(solution)/shard_map/ppermute | solution.py:19
  88.4 10.5 %collective-permute-start.8 = (bf16[256,512]{1,0:T(8,128)(2,1)S(1)}, bf16[256,512]{1,0:T(8,128)(2,1)S(1)}, u32[]{:S(2)}, u32[]{:S(2)}) collective-permute-start(bf16[256,512]{1,0:T(8,128)(2,1)S(1)} %collective-permute-done.7.refs_7_), channel_id=1, source_target_pairs={{48,0},{0,16},{16,32},{32,48},{49,1},{1,17},{17,33},{33,49},{50,2}... | collective-permute-start | bytes 786440 | tf_op jit(solution)/shard_map/ppermute | solution.py:19
  89.3 19.2 %collective-permute-start.29 = (bf16[32,2304]{1,0:T(8,128)(2,1)S(1)}, bf16[32,2304]{1,0:T(8,128)(2,1)S(1)}, u32[]{:S(2)}, u32[]{:S(2)}) collective-permute-start(bf16[32,2304]{1,0:T(8,128)(2,1)S(1)} %get-tuple-element.78), channel_id=1, source_target_pairs={{2,0},{4,2},{6,4},{0,6},{3,1},{5,3},{7,5},{1,7},{10,8},{12,10},{14... | collective-permute-start | bytes 442376 | tf_op jit(solution)/shard_map/ppermute | solution.py:19
  108.3 15.5 %collective-permute-start.10 = (bf16[256,2304]{1,0:T(8,128)(2,1)}, bf16[256,2304]{1,0:T(8,128)(2,1)S(1)}, u32[]{:S(2)}, u32[]{:S(2)}) collective-permute-start(bf16[256,2304]{1,0:T(8,128)(2,1)} %get-tuple-element.41), channel_id=1, source_target_pairs={{1,0},{0,1},{3,2},{2,3},{5,4},{4,5},{7,6},{6,7},{9,8},{8,9},{11,10... | collective-permute-start | bytes 3538952 | tf_op jit(solution)/shard_map/ppermute | solution.py:19
  108.3 15.5 %collective-permute-start.27 = (bf16[64,2304]{1,0:T(8,128)(2,1)S(1)}, bf16[64,2304]{1,0:T(8,128)(2,1)S(1)}, u32[]{:S(2)}, u32[]{:S(2)}) collective-permute-start(bf16[64,2304]{1,0:T(8,128)(2,1)S(1)} %get-tuple-element.75), channel_id=1, source_target_pairs={{6,0},{0,2},{2,4},{4,6},{7,1},{1,3},{3,5},{5,7},{14,8},{8,10},{10,... | collective-permute-start | bytes 884744 | tf_op jit(solution)/shard_map/ppermute | solution.py:19
  108.4 22.5 %copy-start.11 = (bf16[256,2304]{1,0:T(8,128)(2,1)S(1)}, bf16[256,2304]{1,0:T(8,128)(2,1)}, u32[]{:S(2)}) copy-start(bf16[256,2304]{1,0:T(8,128)(2,1)} %get-tuple-element.40) | copy-start | bytes 3538948
  108.4 13.7 %collective-permute-start.25 = (bf16[32,2304]{1,0:T(8,128)(2,1)S(1)}, bf16[32,2304]{1,0:T(8,128)(2,1)S(1)}, u32[]{:S(2)}, u32[]{:S(2)}) collective-permute-start(bf16[32,2304]{1,0:T(8,128)(2,1)S(1)} %get-tuple-element.77), channel_id=1, source_target_pairs={{6,0},{0,2},{2,4},{4,6},{7,1},{1,3},{3,5},{5,7},{14,8},{8,10},{10,... | collective-permute-start | bytes 442376 | tf_op jit(solution)/shard_map/ppermute | solution.py:19
  108.6 15.2 %collective-permute-start.30 = (bf16[64,2304]{1,0:T(8,128)(2,1)S(1)}, bf16[64,2304]{1,0:T(8,128)(2,1)S(1)}, u32[]{:S(2)}, u32[]{:S(2)}) collective-permute-start(bf16[64,2304]{1,0:T(8,128)(2,1)S(1)} %pad_maximum_fusion.3), channel_id=1, source_target_pairs={{2,0},{4,2},{6,4},{0,6},{3,1},{5,3},{7,5},{1,7},{10,8},{12,10},{14... | collective-permute-start | bytes 884744 | tf_op jit(solution)/shard_map/ppermute | solution.py:19
  122.2 8.7 %collective-permute-start.26 = (bf16[64,2304]{1,0:T(8,128)(2,1)S(1)}, bf16[64,2304]{1,0:T(8,128)(2,1)S(1)}, u32[]{:S(2)}, u32[]{:S(2)}) collective-permute-start(bf16[64,2304]{1,0:T(8,128)(2,1)S(1)} %pad_maximum_fusion.2), channel_id=1, source_target_pairs={{8,0},{0,8},{9,1},{1,9},{10,2},{2,10},{11,3},{3,11},{12,4},{4,12},... | collective-permute-start | bytes 884744 | tf_op jit(solution)/shard_map/ppermute | solution.py:19
  132.1 8.1 %collective-permute-start.31 = (bf16[64,2304]{1,0:T(8,128)(2,1)}, bf16[64,2304]{1,0:T(8,128)(2,1)}, u32[]{:S(2)}, u32[]{:S(2)}) collective-permute-start(bf16[64,2304]{1,0:T(8,128)(2,1)} %get-tuple-element.71), channel_id=1, source_target_pairs={{8,0},{0,8},{9,1},{1,9},{10,2},{2,10},{11,3},{3,11},{12,4},{4,12},... | collective-permute-start | bytes 884744 | tf_op jit(solution)/shard_map/ppermute | solution.py:19
  133.6 9.0 %collective-permute-start.28 = (bf16[64,2304]{1,0:T(8,128)(2,1)}, bf16[64,2304]{1,0:T(8,128)(2,1)}, u32[]{:S(2)}, u32[]{:S(2)}) collective-permute-start(bf16[64,2304]{1,0:T(8,128)(2,1)} %get-tuple-element.72), channel_id=1, source_target_pairs={{6,0},{0,2},{2,4},{4,6},{7,1},{1,3},{3,5},{5,7},{14,8},{8,10},{10,... | collective-permute-start | bytes 884744 | tf_op jit(solution)/shard_map/ppermute | solution.py:19
  133.6 9.0 %collective-permute-start.11 = (bf16[64,2304]{1,0:T(8,128)(2,1)}, bf16[64,2304]{1,0:T(8,128)(2,1)}, u32[]{:S(2)}, u32[]{:S(2)}) collective-permute-start(bf16[64,2304]{1,0:T(8,128)(2,1)} %get-tuple-element.70), channel_id=1, source_target_pairs={{2,0},{4,2},{6,4},{0,6},{3,1},{5,3},{7,5},{1,7},{10,8},{12,10},{14... | collective-permute-start | bytes 884744 | tf_op jit(solution)/shard_map/ppermute | solution.py:19
  144.0 7.3 %collective-permute-start.33 = (bf16[64,2304]{1,0:T(8,128)(2,1)S(1)}, bf16[64,2304]{1,0:T(8,128)(2,1)S(1)}, u32[]{:S(2)}, u32[]{:S(2)}) collective-permute-start(bf16[64,2304]{1,0:T(8,128)(2,1)S(1)} %multiply_convert_fusion), channel_id=1, source_target_pairs={{2,0},{4,2},{6,4},{0,6},{3,1},{5,3},{7,5},{1,7},{10,8},{12,10},{14... | collective-permute-start | bytes 884744 | tf_op jit(solution)/shard_map/ppermute | solution.py:19
  147.1 9.7 %collective-permute-start.32 = (bf16[64,2304]{1,0:T(8,128)(2,1)S(1)}, bf16[64,2304]{1,0:T(8,128)(2,1)S(1)}, u32[]{:S(2)}, u32[]{:S(2)}) collective-permute-start(bf16[64,2304]{1,0:T(8,128)(2,1)S(1)} %multiply_convert_fusion), channel_id=1, source_target_pairs={{8,0},{0,8},{9,1},{1,9},{10,2},{2,10},{11,3},{3,11},{12,4},{4,12},... | collective-permute-start | bytes 884744 | tf_op jit(solution)/shard_map/ppermute | solution.py:19
  147.6 9.6 %collective-permute-start.34 = (bf16[64,2304]{1,0:T(8,128)(2,1)S(1)}, bf16[64,2304]{1,0:T(8,128)(2,1)S(1)}, u32[]{:S(2)}, u32[]{:S(2)}) collective-permute-start(bf16[64,2304]{1,0:T(8,128)(2,1)S(1)} %multiply_convert_fusion), channel_id=1, source_target_pairs={{6,0},{0,2},{2,4},{4,6},{7,1},{1,3},{3,5},{5,7},{14,8},{8,10},{10,... | collective-permute-start | bytes 884744 | tf_op jit(solution)/shard_map/ppermute | solution.py:19
  151.3 8.9 %collective-permute-start.42 = (bf16[64,2304]{1,0:T(8,128)(2,1)S(1)}, bf16[64,2304]{1,0:T(8,128)(2,1)S(1)}, u32[]{:S(2)}, u32[]{:S(2)}) collective-permute-start(bf16[64,2304]{1,0:T(8,128)(2,1)S(1)} %collective-permute-done.33), channel_id=1, source_target_pairs={{8,0},{0,8},{9,1},{1,9},{10,2},{2,10},{11,3},{3,11},{12,4},{4,12},... | collective-permute-start | bytes 884744 | tf_op jit(solution)/shard_map/ppermute | solution.py:19
  156.7 8.0 %collective-permute-start.43 = (bf16[64,2304]{1,0:T(8,128)(2,1)S(1)}, bf16[64,2304]{1,0:T(8,128)(2,1)S(1)}, u32[]{:S(2)}, u32[]{:S(2)}) collective-permute-start(bf16[64,2304]{1,0:T(8,128)(2,1)S(1)} %collective-permute-done.32), channel_id=1, source_target_pairs={{6,0},{0,2},{2,4},{4,6},{7,1},{1,3},{3,5},{5,7},{14,8},{8,10},{10,... | collective-permute-start | bytes 884744 | tf_op jit(solution)/shard_map/ppermute | solution.py:19
  157.3 13.0 %copy-start.12 = (bf16[256,2304]{1,0:T(8,128)(2,1)}, bf16[256,2304]{1,0:T(8,128)(2,1)S(1)}, u32[]{:S(2)}) copy-start(bf16[256,2304]{1,0:T(8,128)(2,1)S(1)} %pad_maximum_fusion.1.refs_0_) | copy-start | bytes 3538948
  157.3 14.1 %collective-permute-start.35 = (bf16[256,2304]{1,0:T(8,128)(2,1)S(1)}, bf16[256,2304]{1,0:T(8,128)(2,1)S(1)}, u32[]{:S(2)}, u32[]{:S(2)}) collective-permute-start(bf16[256,2304]{1,0:T(8,128)(2,1)S(1)} %pad_maximum_fusion.1.refs_0_), channel_id=1, source_target_pairs={{1,0},{0,1},{3,2},{2,3},{5,4},{4,5},{7,6},{6,7},{9,8},{8,9},{11,10... | collective-permute-start | bytes 3538952 | tf_op jit(solution)/shard_map/ppermute | solution.py:19
  157.4 10.2 %collective-permute-start.44 = (bf16[64,2304]{1,0:T(8,128)(2,1)S(1)}, bf16[64,2304]{1,0:T(8,128)(2,1)S(1)}, u32[]{:S(2)}, u32[]{:S(2)}) collective-permute-start(bf16[64,2304]{1,0:T(8,128)(2,1)S(1)} %collective-permute-done.33), channel_id=1, source_target_pairs={{2,0},{4,2},{6,4},{0,6},{3,1},{5,3},{7,5},{1,7},{10,8},{12,10},{14... | collective-permute-start | bytes 884744 | tf_op jit(solution)/shard_map/ppermute | solution.py:19
  160.2 10.0 %collective-permute-start.45 = (bf16[32,2304]{1,0:T(8,128)(2,1)S(1)}, bf16[32,2304]{1,0:T(8,128)(2,1)S(1)}, u32[]{:S(2)}, u32[]{:S(2)}) collective-permute-start(bf16[32,2304]{1,0:T(8,128)(2,1)S(1)} %slice.124), channel_id=1, source_target_pairs={{2,0},{4,2},{6,4},{0,6},{3,1},{5,3},{7,5},{1,7},{10,8},{12,10},{14... | collective-permute-start | bytes 442376 | tf_op jit(solution)/shard_map/ppermute | solution.py:19
  164.7 6.6 %collective-permute-start.46 = (bf16[32,2304]{1,0:T(8,128)(2,1)S(1)}, bf16[32,2304]{1,0:T(8,128)(2,1)S(1)}, u32[]{:S(2)}, u32[]{:S(2)}) collective-permute-start(bf16[32,2304]{1,0:T(8,128)(2,1)S(1)} %slice.125), channel_id=1, source_target_pairs={{6,0},{0,2},{2,4},{4,6},{7,1},{1,3},{3,5},{5,7},{14,8},{8,10},{10,... | collective-permute-start | bytes 442376 | tf_op jit(solution)/shard_map/ppermute | solution.py:19
  171.3 23.9 %collective-permute-start.47 = (bf16[256,2304]{1,0:T(8,128)(2,1)S(1)}, bf16[256,2304]{1,0:T(8,128)(2,1)S(1)}, u32[]{:S(2)}, u32[]{:S(2)}) collective-permute-start(bf16[256,2304]{1,0:T(8,128)(2,1)S(1)} %constant_dynamic-update-slice_fusion.5.refs_0_), channel_id=1, source_target_pairs={{1,0},{0,1},{3,2},{2,3},{5,4},{4,5},{7,6},{6,7},{9,8},{8,9},{11,10... | collective-permute-start | bytes 3538952 | tf_op jit(solution)/shard_map/ppermute | solution.py:19
  181.5 9.4 %collective-permute-start.40 = (bf16[256,512]{1,0:T(8,128)(2,1)}, bf16[256,512]{1,0:T(8,128)(2,1)S(1)}, u32[]{:S(2)}, u32[]{:S(2)}) collective-permute-start(bf16[256,512]{1,0:T(8,128)(2,1)} %get-tuple-element.53), channel_id=1, source_target_pairs={{16,0},{32,16},{48,32},{0,48},{17,1},{33,17},{49,33},{1,49},{18,2}... | collective-permute-start | bytes 786440 | tf_op jit(solution)/shard_map/ppermute | solution.py:19
  182.5 11.6 %collective-permute-start.36 = (bf16[256,512]{1,0:T(8,128)(2,1)}, bf16[256,512]{1,0:T(8,128)(2,1)S(1)}, u32[]{:S(2)}, u32[]{:S(2)}) collective-permute-start(bf16[256,512]{1,0:T(8,128)(2,1)} %get-tuple-element.48), channel_id=1, source_target_pairs={{48,0},{0,16},{16,32},{32,48},{49,1},{1,17},{17,33},{33,49},{50,2}... | collective-permute-start | bytes 786440 | tf_op jit(solution)/shard_map/ppermute | solution.py:19
  183.5 41.0 %collective-permute-start.39 = (bf16[256,512]{1,0:T(8,128)(2,1)}, bf16[256,512]{1,0:T(8,128)(2,1)S(1)}, u32[]{:S(2)}, u32[]{:S(2)}) collective-permute-start(bf16[256,512]{1,0:T(8,128)(2,1)} %get-tuple-element.51), channel_id=1, source_target_pairs={{48,0},{0,16},{16,32},{32,48},{49,1},{1,17},{17,33},{33,49},{50,2}... | collective-permute-start | bytes 786440 | tf_op jit(solution)/shard_map/ppermute | solution.py:19
  184.0 53.9 %collective-permute-start.38 = (bf16[256,512]{1,0:T(8,128)(2,1)}, bf16[256,512]{1,0:T(8,128)(2,1)S(1)}, u32[]{:S(2)}, u32[]{:S(2)}) collective-permute-start(bf16[256,512]{1,0:T(8,128)(2,1)} %get-tuple-element.49), channel_id=1, source_target_pairs={{16,0},{32,16},{48,32},{0,48},{17,1},{33,17},{49,33},{1,49},{18,2}... | collective-permute-start | bytes 786440 | tf_op jit(solution)/shard_map/ppermute | solution.py:19
  191.8 32.8 %collective-permute-start.41 = (bf16[256,512]{1,0:T(8,128)(2,1)S(1)}, bf16[256,512]{1,0:T(8,128)(2,1)S(1)}, u32[]{:S(2)}, u32[]{:S(2)}) collective-permute-start(bf16[256,512]{1,0:T(8,128)(2,1)S(1)} %add_convert_fusion.9), channel_id=1, source_target_pairs={{16,0},{32,16},{48,32},{0,48},{17,1},{33,17},{49,33},{1,49},{18,2}... | collective-permute-start | bytes 786440 | tf_op jit(solution)/shard_map/ppermute | solution.py:19
  195.1 45.6 %collective-permute-start.37 = (bf16[256,512]{1,0:T(8,128)(2,1)S(1)}, bf16[256,512]{1,0:T(8,128)(2,1)S(1)}, u32[]{:S(2)}, u32[]{:S(2)}) collective-permute-start(bf16[256,512]{1,0:T(8,128)(2,1)S(1)} %add_convert_fusion.10), channel_id=1, source_target_pairs={{48,0},{0,16},{16,32},{32,48},{49,1},{1,17},{17,33},{33,49},{50,2}... | collective-permute-start | bytes 786440 | tf_op jit(solution)/shard_map/ppermute | solution.py:19
  205.2 19.9 %collective-permute-start.52 = (bf16[256,512]{1,0:T(8,128)(2,1)}, bf16[256,512]{1,0:T(8,128)(2,1)S(1)}, u32[]{:S(2)}, u32[]{:S(2)}) collective-permute-start(bf16[256,512]{1,0:T(8,128)(2,1)} %get-tuple-element.63), channel_id=1, source_target_pairs={{16,0},{32,16},{48,32},{0,48},{17,1},{33,17},{49,33},{1,49},{18,2}... | collective-permute-start | bytes 786440 | tf_op jit(solution)/shard_map/ppermute | solution.py:19
  224.5 13.3 %copy-start.22 = (bf16[256,512]{1,0:T(8,128)(2,1)S(1)}, bf16[256,512]{1,0:T(8,128)(2,1)}, u32[]{:S(2)}) copy-start(bf16[256,512]{1,0:T(8,128)(2,1)} %get-tuple-element.57) | copy-start | bytes 786436
  224.5 18.3 %collective-permute-start.51 = (bf16[256,512]{1,0:T(8,128)(2,1)S(1)}, bf16[256,512]{1,0:T(8,128)(2,1)S(1)}, u32[]{:S(2)}, u32[]{:S(2)}) collective-permute-start(bf16[256,512]{1,0:T(8,128)(2,1)S(1)} %copy-done.29), channel_id=1, source_target_pairs={{48,0},{0,16},{16,32},{32,48},{49,1},{1,17},{17,33},{33,49},{50,2}... | collective-permute-start | bytes 786440 | tf_op jit(solution)/shard_map/ppermute | solution.py:19
  224.7 13.2 %collective-permute-start.48 = (bf16[256,512]{1,0:T(8,128)(2,1)S(1)}, bf16[256,512]{1,0:T(8,128)(2,1)S(1)}, u32[]{:S(2)}, u32[]{:S(2)}) collective-permute-start(bf16[256,512]{1,0:T(8,128)(2,1)S(1)} %copy-done.38), channel_id=1, source_target_pairs={{48,0},{0,16},{16,32},{32,48},{49,1},{1,17},{17,33},{33,49},{50,2}... | collective-permute-start | bytes 786440 | tf_op jit(solution)/shard_map/ppermute | solution.py:19
  225.0 17.8 %copy-start.18 = (bf16[256,512]{1,0:T(8,128)(2,1)S(1)}, bf16[256,512]{1,0:T(8,128)(2,1)}, u32[]{:S(2)}) copy-start(bf16[256,512]{1,0:T(8,128)(2,1)} %get-tuple-element.46) | copy-start | bytes 786436
  225.5 18.8 %collective-permute-start.50 = (bf16[256,512]{1,0:T(8,128)(2,1)S(1)}, bf16[256,512]{1,0:T(8,128)(2,1)S(1)}, u32[]{:S(2)}, u32[]{:S(2)}) collective-permute-start(bf16[256,512]{1,0:T(8,128)(2,1)S(1)} %copy-done.28), channel_id=1, source_target_pairs={{16,0},{32,16},{48,32},{0,48},{17,1},{33,17},{49,33},{1,49},{18,2}... | collective-permute-start | bytes 786440 | tf_op jit(solution)/shard_map/ppermute | solution.py:19
  228.4 15.8 %copy-start.21 = (bf16[256,512]{1,0:T(8,128)(2,1)S(1)}, bf16[256,512]{1,0:T(8,128)(2,1)}, u32[]{:S(2)}) copy-start(bf16[256,512]{1,0:T(8,128)(2,1)} %get-tuple-element.60) | copy-start | bytes 786436
  237.8 6.4 %collective-permute-start.53 = (bf16[256,512]{1,0:T(8,128)(2,1)S(1)}, bf16[256,512]{1,0:T(8,128)(2,1)S(1)}, u32[]{:S(2)}, u32[]{:S(2)}) collective-permute-start(bf16[256,512]{1,0:T(8,128)(2,1)S(1)} %add_convert_fusion.7), channel_id=1, source_target_pairs={{16,0},{32,16},{48,32},{0,48},{17,1},{33,17},{49,33},{1,49},{18,2}... | collective-permute-start | bytes 786440 | tf_op jit(solution)/shard_map/ppermute | solution.py:19
  237.9 212.5 %collective-permute-start.56 = (bf16[2880,512]{1,0:T(8,128)(2,1)}, bf16[2880,512]{1,0:T(8,128)(2,1)}, u32[]{:S(2)}, u32[]{:S(2)}) collective-permute-start(bf16[2880,512]{1,0:T(8,128)(2,1)} %constant_dynamic-slice_fusion), channel_id=1, source_target_pairs={{64,0},{0,64},{65,1},{1,65},{66,2},{2,66},{67,3},{3,67},{68,4},{4,... | collective-permute-start | bytes 8847368 | tf_op jit(solution)/shard_map/ppermute | solution.py:19
  240.7 7.6 %collective-permute-start.49 = (bf16[256,512]{1,0:T(8,128)(2,1)S(1)}, bf16[256,512]{1,0:T(8,128)(2,1)S(1)}, u32[]{:S(2)}, u32[]{:S(2)}) collective-permute-start(bf16[256,512]{1,0:T(8,128)(2,1)S(1)} %add_convert_fusion.8), channel_id=1, source_target_pairs={{48,0},{0,16},{16,32},{32,48},{49,1},{1,17},{17,33},{33,49},{50,2}... | collective-permute-start | bytes 786440 | tf_op jit(solution)/shard_map/ppermute | solution.py:19
  252.9 194.9 %collective-permute-start.54 = (bf16[1152,512]{1,0:T(8,128)(2,1)}, bf16[1152,512]{1,0:T(8,128)(2,1)}, u32[]{:S(2)}, u32[]{:S(2)}) collective-permute-start(bf16[1152,512]{1,0:T(8,128)(2,1)} %constant_dynamic-slice_fusion.1), channel_id=1, source_target_pairs={{64,0},{0,64},{65,1},{1,65},{66,2},{2,66},{67,3},{3,67},{68,4},{4,... | collective-permute-start | bytes 3538952 | tf_op jit(solution)/shard_map/ppermute | solution.py:19
  442.0 5.2 %collective-permute-start.55 = (f32[512]{0:T(512)S(1)}, f32[512]{0:T(512)S(1)}, u32[]{:S(2)}, u32[]{:S(2)}) collective-permute-start(f32[512]{0:T(512)S(1)} %add.145), channel_id=1, source_target_pairs={{64,0},{0,64},{65,1},{1,65},{66,2},{2,66},{67,3},{3,67},{68,4},{4,... | collective-permute-start | bytes 6152 | tf_op jit(solution)/shard_map/ppermute | solution.py:19
  (34 other events, 116.7 us)
